TPU v7x, 256 devices: a whole 4x4x8 slice. The times are simulated.
256 devices in a mesh: ex: 32 (over x, z), feat: 8 (over y, core).
Axes of the slice: x: 4, y: 4, z: 8, core: 2. Of those that a mesh axis runs over, the one named last changes fastest.
Arguments:
- train_grads: bfloat16 [16384, 32768], P('ex', 'feat'), may hold values from -0.03125 to 0.03125
- audit_grads: bfloat16 [2, 32, 32, 32768], P(None, 'ex', None, 'feat'), may hold values from -6 to 6
- owner_map: int32 [64], replicated, may hold values from 0 to 63, as said below
- pair_blocks: int32 [32, 32], P('ex'), may hold values from 0 to 63, as said below
- pair_counts: int32 [32], P('ex'), may hold values from 1 to 32, as said below
Outputs:
- tiles: float32 [32, 32, 32, 512], P('ex', 'feat')
Inputs may be any that keep to these rules, and one draw needn't show every extreme that they name: `owner_map`: a permutation of the audit blocks. `pair_blocks`: the 32 entries of each training block name audit blocks whose stored blocks lie on 32 different indices of ex (owner_map[a] % 32 differs); entries at or after pair_counts are not live. `pair_counts`: some training block has all 32 pairs live.
All inputs are finite; a program needn't handle non-finite values.
Results may differ from a plain program's by a relative error of at most 0.0003.
Values may be sent and summed in bfloat16 or wider, within the bound.
A program may use at most 64 MiB of HBM per device.

v0:
```python
import jax
import jax.numpy as jnp
from jax import lax
from jax.sharding import PartitionSpec as P


def shards(train_grads, audit_grads, owner_map, pair_blocks, pair_counts):
    peers = lax.axis_size("ex")
    stored = jnp.take(owner_map, pair_blocks[0])
    holder = stored % peers
    local = stored // peers
    order = jnp.arange(peers, dtype=jnp.int32)
    live = (order < pair_counts[0]).astype(jnp.float32)
    stored_count = audit_grads.shape[0]
    piece = lax.all_gather(audit_grads, "ex", axis=1, tiled=True)
    count = piece.shape[1]
    scores = jnp.einsum("jnaf,tf->jnat", piece, train_grads, preferred_element_type=jnp.float32)
    span = jnp.arange(count, dtype=jnp.int32)
    kinds = jnp.arange(stored_count, dtype=jnp.int32)
    pick = (
        (local[:, None, None] == kinds[None, :, None])
        & (holder[:, None, None] == span[None, None, :])
    ).astype(jnp.float32)
    summed = jnp.einsum("kjn,jnat->kat", pick, scores, precision=lax.Precision.HIGHEST)
    tiles = lax.psum_scatter(summed * live[:, None, None], "feat", scatter_dimension=0, tiled=True)
    return tiles[None]


def solution(mesh):
    in_specs = (P("ex", "feat"), P(None, "ex", None, "feat"), P(), P("ex", None), P("ex"))
    out_specs = P("ex", "feat", None, None)
    return jax.shard_map(shards, mesh=mesh, in_specs=in_specs, out_specs=out_specs, check_vma=False)
```

profile of v0, /device:TPU:2, one launch (start us, length us, event | category | flops | bytes accessed | tf_op | source)
XLA Modules:
  0.0 212.7 jit_solution(17355145147538234622)
XLA Ops:
  6.5 0.0 copy-start
  6.5 0.0 all-gather.2.cloned.1.call-start
  6.5 0.7 all-gather.2.cloned.1.call-update
  7.3 0.0 reduce-scatter.2.cloned.1.call-start
  8.0 0.7 fusion.10
  8.6 0.0 copy-done
  8.6 0.7 gather_fusion
  9.3 0.7 and_select_fusion.1
  10.0 0.1 iota_compare_fusion
  10.1 141.2 %all-gather.2.cloned.1.call-done = bf16[2,32,32,4096]{3,2,1,0:T(8,128)(2,1)} async-done(((bf16[2,1,32,4096]{3,2,1,0:T(8,128)(2,1)}), bf16[2,32,32,4096]{3,2,1,0:T(8,128)(2,1)}) %all-gather.2.cloned.1.call-update) | async-done | bytes 16777232 | tf_op jit(solution)/shard_map/all_gather | solution.py:15
  151.3 13.0 %fusion = f32[2,32,32,512]{3,2,1,0:T(8,128)S(1)} fusion(bf16[2,32,32,4096]{3,2,1,0:T(8,128)(2,1)} %all-gather.2.cloned.1.call-done, bf16[512,4096]{1,0:T(8,128)(2,1)} %param.5), kind=kOutput, calls=%fused_computation.1 | convolution fusion | flops 8589934592 | bytes 25165824 | tf_op jit(solution)/shard_map/jnaf,tf->jnat/dot_general | solution.py:17
  164.3 4.1 %bitcast_multiply_fusion = f32[32,32,512]{2,0,1:T(8,128)S(1)} fusion(f32[2,32,32,512]{3,2,1,0:T(8,128)S(1)} %fusion, f32[32]{0:T(128)S(1)} %compare_convert_fusion, pred[32,32]{1,0:T(8,128)(4,1)S(1)} %iota_compare_fusion, pred[32,2]{0,1:T(4,128)(4,1)S(1)} %iota_compare_fusion.1), kind=kOutput, calls=%fused_computation.5 | convolution fusion | flops 403179520 | bytes 6292672 | tf_op jit(solution)/shard_map/kjn,jnat->kat/dot_general | solution.py:24
  168.4 2.6 %copy.9 = f32[32,32,512]{2,1,0:T(8,128)} copy(f32[32,32,512]{2,0,1:T(8,128)S(1)} %bitcast_multiply_fusion) | data formatting | bytes 4194304 | tf_op jit(solution)/shard_map/mul | solution.py:25
  171.0 0.0 reduce-scatter.2.cloned.1.call-update
  171.0 34.9 %reduce-scatter.2.cloned.1.call-done = f32[4,32,512]{2,1,0:T(8,128)} async-done(((f32[32,32,512]{2,1,0:T(8,128)}), f32[4,32,512]{2,1,0:T(8,128)}) %reduce-scatter.2.cloned.1.call-update) | async-done | bytes 262160 | tf_op jit(solution)/shard_map/reduce_scatter | solution.py:25
  (4 shorter events, 0.0 us)
Async XLA Ops:
  6.5 2.1 copy-start
  6.5 144.8 %all-gather.2.cloned.1.call-start = ((), (), s32[]{:S(2)}) async-start(), calls=%async_computation.1 | async-start | bytes 17301504 | tf_op jit(solution)/shard_map/all_gather | solution.py:15
  7.3 198.6 %reduce-scatter.2.cloned.1.call-start = ((), (), s32[]{:S(2)}) async-start(), calls=%async_computation.2 | async-start | bytes 2359296 | tf_op jit(solution)/shard_map/reduce_scatter | solution.py:25
Sparse Core Ops, SparseCore 0:
  9.9 141.3 all-gather.1
  171.1 34.7 reduce-scatter.1
where the time goes:
time: 213 us
  waiting for transfers between devices  177 us (83%)
  matrix products  17.1 us (8%)
  between operations  14.1 us (7%)
  local copies, waits for them, and re-layouts  3.26 us (2%)
    all_gather x1, waiting for transfers between devices, shards(): piece = lax.all_gather(audit_grads, 'ex', axis=1, tiled=True)  141 us
    reduce_scatter x1, waiting for transfers between devices, shards(): lax.psum_scatter(summed * live[:, None, None], 'feat', scatter_dimension=...  34.9 us
    dot_general x1, matrix products, shards(): jnp.einsum('jnaf,tf->jnat', piece, train_grads, preferred_element_type=jn...  13 us
  transfers between devices with their start and end apart: 2, of which 2 were waited for; matrix products, arithmetic and copies ran while one was open for 1% of the time, Pallas kernels for 0%

commit v1 on v0

--- a/solution.py
+++ b/solution.py
@@ -12,7 +12,10 @@
     order = jnp.arange(peers, dtype=jnp.int32)
     live = (order < pair_counts[0]).astype(jnp.float32)
     stored_count = audit_grads.shape[0]
-    piece = lax.all_gather(audit_grads, "ex", axis=1, tiled=True)
+    seen = []
+    for _ in range(lax.axis_size("ex")):
+        seen.append(audit_grads)
+    piece = jnp.concatenate(lax.all_to_all(jnp.stack(seen, axis=0), "ex", 0, 0), 1)
     count = piece.shape[1]
     scores = jnp.einsum("jnaf,tf->jnat", piece, train_grads, preferred_element_type=jnp.float32)
     span = jnp.arange(count, dtype=jnp.int32)

time: 213 us -> 499 us (2.34)
  waiting for transfers between devices: 177 us -> 446 us
  starting transfers between devices: 0.04 us -> 11.8 us
  local copies, waits for them, and re-layouts: 3.26 us -> 10 us
    all_to_all x0 -> x1, waiting for transfers between devices: none -> 408 us  [shards(): lax.all_to_all(jnp.stack(seen, axis=0), 'ex', 0, 0)]
    all_gather x1 -> x0, waiting for transfers between devices: 141 us -> none  [shards(): piece = lax.all_gather(audit_grads, 'ex', axis=1, tiled=True)]
    all_to_all x0 -> x1, starting transfers between devices: none -> 11.8 us  [shards(): lax.all_to_all(jnp.stack(seen, axis=0), 'ex', 0, 0)]
    another operation x0 -> x1, local copies, waits for them, and re-layouts: none -> 6.74 us  [shards(): jnp.stack(seen, axis=0)]
  transfers between devices with their start and end apart: 2 -> 2, of which waited for: 2 -> 2; matrix products, arithmetic and copies ran while one was open for 1% -> 0% of each run, Pallas kernels for 0% -> 0%
where the time goes in v1:
time: 499 us
  waiting for transfers between devices  446 us (89%)
  matrix products  17.1 us (3%)
  between operations  14.1 us (3%)
  starting transfers between devices  11.8 us (2%)
  local copies, waits for them, and re-layouts  10 us (2%)
    all_to_all x1, waiting for transfers between devices, shards(): lax.all_to_all(jnp.stack(seen, axis=0), 'ex', 0, 0)  408 us
    reduce_scatter x1, waiting for transfers between devices, shards(): lax.psum_scatter(summed * live[:, None, None], 'feat', scatter_dimension=...  38.3 us
    dot_general x1, matrix products, shards(): jnp.einsum('jnaf,tf->jnat', piece, train_grads, preferred_element_type=jn...  13 us
    all_to_all x1, starting transfers between devices, shards(): lax.all_to_all(jnp.stack(seen, axis=0), 'ex', 0, 0)  11.8 us
  transfers between devices with their start and end apart: 2, of which 2 were waited for; matrix products, arithmetic and copies ran while one was open for 0% of the time, Pallas kernels for 0%

profile of v1, /device:TPU:2, one launch (start us, length us, event | category | flops | bytes accessed | tf_op | source)
XLA Modules:
  0.0 499.1 jit_solution(15050060060410629618)
XLA Ops:
  6.5 0.0 copy-start
  6.5 6.7 %stack.2 = bf16[32,2,1,32,4096]{4,3,1,2,0:T(8,128)(2,1)} broadcast(bf16[2,32,4096]{2,1,0:T(8,128)(2,1)} %bitcast.27), dimensions={1,3,4} | broadcast | bytes 17301504 | tf_op jit(solution)/shard_map/stack | solution.py:18
  13.3 0.0 copy-start.1
  13.3 11.8 %all-to-all-start = ((bf16[32,2,1,32,4096]{4,3,1,2,0:T(8,128)(2,1)}), bf16[32,2,1,32,4096]{4,3,1,2,0:T(8,128)(2,1)}, u32[]{:S(2)}, u32[]{:S(2)}) async-start(bf16[32,2,1,32,4096]{4,3,1,2,0:T(8,128)(2,1)} %stack.2), calls=%async_computation | async-start | bytes 33554432 | tf_op jit(solution)/shard_map/all_to_all | solution.py:18
  25.1 0.0 reduce-scatter.2.cloned.1.call-start
  25.8 0.0 copy-done.1
  25.8 0.0 copy-done
  25.8 0.7 gather_fusion
  26.6 0.1 iota_compare_fusion
  26.7 407.7 %all-to-all-done = bf16[32,2,1,32,4096]{4,3,1,2,0:T(8,128)(2,1)} async-done(((bf16[32,2,1,32,4096]{4,3,1,2,0:T(8,128)(2,1)}), bf16[32,2,1,32,4096]{4,3,1,2,0:T(8,128)(2,1)}, u32[]{:S(2)}, u32[]{:S(2)}) %all-to-all-start) | async-done | bytes 16777248 | tf_op jit(solution)/shard_map/all_to_all | solution.py:18
  434.3 13.0 %fusion = f32[2,32,32,512]{3,2,1,0:T(8,128)S(1)} fusion(bf16[32,2,1,32,4096]{4,3,1,2,0:T(8,128)(2,1)} %all-to-all-done, bf16[512,4096]{1,0:T(8,128)(2,1)} %param.5), kind=kOutput, calls=%fused_computation.1 | convolution fusion | flops 8589934592 | bytes 25165824 | tf_op jit(solution)/shard_map/jnaf,tf->jnat/dot_general | solution.py:20
  447.3 4.1 bitcast_multiply_fusion
  451.4 2.6 copy.12
  454.0 0.0 reduce-scatter.2.cloned.1.call-update
  454.0 38.3 %reduce-scatter.2.cloned.1.call-done = f32[4,32,512]{2,1,0:T(8,128)} async-done(((f32[32,32,512]{2,1,0:T(8,128)}), f32[4,32,512]{2,1,0:T(8,128)}) %reduce-scatter.2.cloned.1.call-update) | async-done | bytes 262160 | tf_op jit(solution)/shard_map/reduce_scatter | solution.py:28
  (6 shorter events, 0.0 us)
Async XLA Ops:
  6.5 19.3 %copy-start = (s32[64]{0:T(128)S(1)}, s32[64]{0:T(128)}, u32[]{:S(2)}) copy-start(s32[64]{0:T(128)} %param.7) | copy-start | bytes 772
  13.3 12.5 %copy-start.1 = (s32[1,32]{1,0:T(1,128)S(1)}, s32[1,32]{1,0:T(1,128)}, u32[]{:S(2)}) copy-start(s32[1,32]{1,0:T(1,128)} %param.8) | copy-start | bytes 388
  13.3 421.0 %all-to-all-start = ((bf16[32,2,1,32,4096]{4,3,1,2,0:T(8,128)(2,1)}), bf16[32,2,1,32,4096]{4,3,1,2,0:T(8,128)(2,1)}, u32[]{:S(2)}, u32[]{:S(2)}) async-start(bf16[32,2,1,32,4096]{4,3,1,2,0:T(8,128)(2,1)} %stack.2), calls=%async_computation | async-start | bytes 33554432 | tf_op jit(solution)/shard_map/all_to_all | solution.py:18
  25.1 467.2 %reduce-scatter.2.cloned.1.call-start = ((), (), s32[]{:S(2)}) async-start(), calls=%async_computation.2 | async-start | bytes 2359296 | tf_op jit(solution)/shard_map/reduce_scatter | solution.py:28
Sparse Core Ops, SparseCore 0:
  454.1 38.1 reduce-scatter.1
